TPU v7x, 256 devices: a whole 4x4x8 slice. The times are simulated.
256 devices in a mesh: src: 16 (over y_lo, x, core), rec: 16 (over y_hi, z).
Axes of the slice: x: 4, y: 4 (y_hi: 2, y_lo: 2; y = y_hi * 2 + y_lo), z: 8, core: 2. Of those that a mesh axis runs over, the one named last changes fastest.
Arguments:
- kernel: bfloat16 [2, 32, 4096, 4096], P(None, None, 'src', 'rec'), may hold values from -0.09375 to 0.09375
- focusing: float32 [64, 4096, 128], P(None, ('rec', 'src')), may hold values from -6 to 6
- first_arrival: float32 [64, 4096, 128], P(None, ('rec', 'src')), may hold values from -6 to 6
- onset: int32 [64, 4096], replicated, may hold values from 32 to 127
Outputs:
- upgoing: float32 [64, 4096, 128], P(None, ('src', 'rec'))
- downgoing: float32 [64, 4096, 128], P(None, ('rec', 'src'))
All inputs are finite; a program needn't handle non-finite values.
Results may differ from a plain program's by a relative error of at most 0.0029.
Values may be sent and summed in bfloat16 or wider, within the bound.
No kernel may reach another device: no remote copies, remote signals or barrier semaphores. Data moves between devices by JAX's collectives and lax.ppermute only.
A program may use at most 128 MiB of HBM per device.

v0:
```python
import jax
import jax.numpy as jnp
from jax import lax
from jax.sharding import PartitionSpec as P

HIGH = lax.Precision.HIGHEST


def tables(count, samples, flipped):
    steps = jnp.arange(samples, dtype=jnp.int32)
    if flipped:
        steps = samples - 1 - steps
    waves = jnp.arange(count, dtype=jnp.int32) + 1
    turns = waves[:, None] * steps[None, :] % samples
    angle = turns.astype(jnp.float32) * (2.0 * jnp.pi / samples)
    return (jnp.cos(angle), jnp.sin(angle))


def spectra(traces, cosine, sine):
    real_part = jnp.einsum("pnt,kt->kpn", traces, cosine, precision=HIGH)
    imag_part = -jnp.einsum("pnt,kt->kpn", traces, sine, precision=HIGH)
    return jnp.stack([real_part, imag_part]).astype(jnp.bfloat16)


def synth(stacked, cosine, sine, samples):
    first = jnp.einsum("kpn,kt->pnt", stacked[0], cosine, precision=HIGH)
    second = jnp.einsum("kpn,kt->pnt", stacked[1], sine, precision=HIGH)
    return 2.0 / samples * (first - second)


def onset_masked(values, onset, start, width):
    limits = lax.dynamic_slice_in_dim(onset, start, width, 1)
    times = jnp.arange(values.shape[2], dtype=jnp.int32)
    return times[None, None, :] < limits[:, :, None]


def per_device(kernel, focusing, first_arrival, onset):
    samples = focusing.shape[2]
    count = kernel.shape[1]
    width = focusing.shape[1]
    n_src = lax.axis_size("src")
    n_rec = lax.axis_size("rec")
    src_idx = lax.axis_index("src")
    rec_idx = lax.axis_index("rec")
    cosine, sine = tables(count, samples, False)
    rcosine, rsine = tables(count, samples, True)
    traces = lax.all_gather(focusing, "src", axis=1, tiled=True)
    wavefield_spectrum = spectra(traces, cosine, sine)
    kernel_real = kernel[0]
    kernel_imaginary = kernel[1]
    conv_re = jnp.einsum(
        "hoy,hny->hon", wavefield_spectrum[0], kernel_real, preferred_element_type=jnp.float32
    ) - jnp.einsum(
        "hoy,hny->hon", wavefield_spectrum[1], kernel_imaginary, preferred_element_type=jnp.float32
    )
    conv_im = jnp.einsum(
        "hoy,hny->hon", wavefield_spectrum[0], kernel_imaginary, preferred_element_type=jnp.float32
    ) + jnp.einsum(
        "hoy,hny->hon", wavefield_spectrum[1], kernel_real, preferred_element_type=jnp.float32
    )
    conv = jnp.stack([conv_re, conv_im])
    share = lax.psum_scatter(conv, "rec", scatter_dimension=3, tiled=True)
    start = (src_idx * n_rec + rec_idx) * width
    traces_up = synth(share, cosine, sine, samples)
    upgoing = jnp.where(onset_masked(traces_up, onset, start, width), traces_up, 0.0)
    upgoing_spectrum = lax.all_gather(spectra(upgoing, cosine, sine), "rec", axis=3, tiled=True)
    corr_re = jnp.einsum(
        "alt,ath->alh", upgoing_spectrum[0], kernel_real, preferred_element_type=jnp.float32
    ) + jnp.einsum(
        "alt,ath->alh", upgoing_spectrum[1], kernel_imaginary, preferred_element_type=jnp.float32
    )
    corr_im = jnp.einsum(
        "alt,ath->alh", upgoing_spectrum[1], kernel_real, preferred_element_type=jnp.float32
    ) - jnp.einsum(
        "alt,ath->alh", upgoing_spectrum[0], kernel_imaginary, preferred_element_type=jnp.float32
    )
    corr = lax.psum_scatter(jnp.stack([corr_re, corr_im]), "src", scatter_dimension=3, tiled=True)
    reversed_part = synth(corr, rcosine, rsine, samples)
    start_down = (rec_idx * n_src + src_idx) * width
    downgoing = first_arrival - jnp.where(
        onset_masked(reversed_part, onset, start_down, width), reversed_part, 0.0
    )
    return (upgoing, downgoing)


def solution(mesh):
    in_specs = (
        P(None, None, "src", "rec"),
        P(None, ("rec", "src"), None),
        P(None, ("rec", "src"), None),
        P(),
    )
    out_specs = (P(None, ("src", "rec"), None), P(None, ("rec", "src"), None))
    return jax.shard_map(
        per_device, mesh=mesh, in_specs=in_specs, out_specs=out_specs, check_vma=False
    )
```

profile of v0, /device:TPU:32, one launch (start us, length us, event | category | flops | bytes accessed | tf_op | source)
XLA Modules:
  0.0 553.0 jit_solution(9216155911850107133)
XLA Ops:
  7.2 0.0 all-gather.3.cloned.1.call-start
  7.2 0.7 all-gather.3.cloned.1.call-update
  7.9 0.0 reduce-scatter.3.cloned.1.call-start
  8.0 59.1 %all-gather.3.cloned.1.call-done = f32[64,256,128]{2,1,0:T(8,128)} async-done(((f32[64,16,128]{2,1,0:T(8,128)}), f32[64,256,128]{2,1,0:T(8,128)}) %all-gather.3.cloned.1.call-update) | async-done | bytes 8388624 | tf_op jit(solution)/shard_map/all_gather | solution.py:47
  67.0 12.0 %negate_convert_fusion = bf16[32,64,256]{2,0,1:T(8,128)(2,1)S(1)} fusion(f32[64,256,128]{2,1,0:T(8,128)} %all-gather.3.cloned.1.call-done, s32[32]{0:T(128)S(1)} %iota_add_fusion), kind=kOutput, calls=%fused_computation.32 | convolution fusion | flops 806412288 | bytes 9437312 | tf_op jit(solution)/shard_map/pnt,kt->kpn/dot_general | solution.py:21
  79.1 1.3 fusion.6
  80.3 8.8 %convolution_convert_fusion = bf16[32,64,256]{2,0,1:T(8,128)(2,1)S(1)} fusion(f32[64,256,128]{2,1,0:T(8,128)S(1)} %copy-done.1, s32[32]{0:T(128)S(1)} %iota_add_fusion), kind=kOutput, calls=%fused_computation.33 | convolution fusion | flops 805888000 | bytes 9437312 | tf_op jit(solution)/shard_map/pnt,kt->kpn/dot_general | solution.py:20
  89.1 1.3 fusion.4
  90.4 1.3 subtract_bitcast_fusion.1
  91.7 1.3 add_bitcast_fusion.1
  93.0 2.3 pad_maximum_fusion
  95.3 9.2 %copy.24 = f32[2,32,64,256]{2,1,0,3:T(8,128)} copy(f32[2,32,64,256]{3,2,1,0:T(8,128)} %pad_maximum_fusion) | data formatting | bytes 8388608 | tf_op jit(solution)/shard_map/stack | solution.py:61
  104.5 0.0 reduce-scatter.3.cloned.1.call-update
  104.5 0.0 all-gather.5.cloned.1.call-start
  104.5 0.9 constant_dynamic-slice_fusion
  105.4 224.5 %reduce-scatter.3.cloned.1.call-done = f32[2,32,64,16]{2,1,0,3:T(8,128)} async-done(((f32[2,32,64,256]{2,1,0,3:T(8,128)}), f32[2,32,64,16]{2,1,0,3:T(8,128)}) %reduce-scatter.3.cloned.1.call-update) | async-done | bytes 262160 | tf_op jit(solution)/shard_map/reduce_scatter | solution.py:62
  329.9 1.1 fusion.114
  330.9 0.3 copy.36
  331.2 0.7 fusion.48
  331.9 0.3 copy.37
  332.2 0.7 fusion.36
  332.9 0.0 copy-start.3
  333.0 1.6 fusion.38
  334.6 0.0 copy-done.3
  334.6 1.6 fusion.39
  336.2 0.8 pad_maximum_fusion.2
  337.0 0.0 all-gather.5.cloned.1.call-update
  337.0 0.3 reduce-scatter.5.cloned.1.call-start
  337.3 98.7 %all-gather.5.cloned.1.call-done = bf16[2,32,64,256]{2,1,3,0:T(8,128)(2,1)} async-done(((bf16[2,32,64,16]{2,1,3,0:T(8,128)(2,1)}), bf16[2,32,64,256]{2,1,3,0:T(8,128)(2,1)}) %all-gather.5.cloned.1.call-update) | async-done | bytes 2097168 | tf_op jit(solution)/shard_map/all_gather | solution.py:66
  436.0 4.3 slice_bitcast_fusion
  440.3 1.7 copy.30
  441.9 4.4 fusion.2
  446.3 2.8 copy.29
  449.1 0.0 slice-start
  449.1 3.2 fusion
  452.3 0.0 slice-start.1
  452.3 3.2 add_bitcast_fusion
  455.5 0.5 slice-done.1
  456.0 0.8 subtract_bitcast_fusion
  456.8 2.3 pad_maximum_fusion.1
  459.1 9.2 %copy.33 = f32[2,32,64,256]{2,1,0,3:T(8,128)} copy(f32[2,32,64,256]{3,2,1,0:T(8,128)} %pad_maximum_fusion.1) | data formatting | bytes 8388608 | tf_op jit(solution)/shard_map/stack | solution.py:77
  468.2 0.0 reduce-scatter.5.cloned.1.call-update
  468.3 74.3 %reduce-scatter.5.cloned.1.call-done = f32[2,32,64,16]{2,1,0,3:T(8,128)} async-done(((f32[2,32,64,256]{2,1,0,3:T(8,128)}), f32[2,32,64,16]{2,1,0,3:T(8,128)}) %reduce-scatter.5.cloned.1.call-update) | async-done | bytes 262160 | tf_op jit(solution)/shard_map/reduce_scatter | solution.py:77
  542.6 1.1 fusion.113
  543.7 0.3 copy.38
  544.0 0.3 copy.39
  544.3 0.7 fusion.45
  545.0 1.5 fusion.34
  (12 shorter events, 0.0 us)
Async XLA Ops:
  7.2 59.8 %all-gather.3.cloned.1.call-start = ((), (), s32[]{:S(2)}) async-start(), calls=%async_computation.2 | async-start | bytes 8912896 | tf_op jit(solution)/shard_map/all_gather | solution.py:47
  7.9 322.0 %reduce-scatter.3.cloned.1.call-start = ((), (), s32[]{:S(2)}) async-start(), calls=%async_computation.3 | async-start | bytes 8912896 | tf_op jit(solution)/shard_map/reduce_scatter | solution.py:62
  67.0 12.0 %copy-start = (bf16[2,32,256,256]{3,2,1,0:T(8,128)(2,1)S(1)}, bf16[2,32,256,256]{3,2,1,0:T(8,128)(2,1)}, u32[]{:S(2)}) copy-start(bf16[2,32,256,256]{3,2,1,0:T(8,128)(2,1)} %param.4) | copy-start | bytes 25165828
  67.0 13.3 %copy-start.1 = (f32[64,256,128]{2,1,0:T(8,128)S(1)}, f32[64,256,128]{2,1,0:T(8,128)}, u32[]{:S(2)}) copy-start(f32[64,256,128]{2,1,0:T(8,128)} %all-gather.3.cloned.1.call-done) | copy-start | bytes 25165828
  104.5 331.5 %all-gather.5.cloned.1.call-start = ((), (), s32[]{:S(2)}) async-start(), calls=%async_computation.4 | async-start | bytes 4456448 | tf_op jit(solution)/shard_map/all_gather | solution.py:66
  332.9 1.7 copy-start.3
  337.0 205.6 %reduce-scatter.5.cloned.1.call-start = ((), (), s32[]{:S(2)}) async-start(), calls=%async_computation.5 | async-start | bytes 8912896 | tf_op jit(solution)/shard_map/reduce_scatter | solution.py:77
  449.1 3.2 copy-start.2
  449.1 6.4 %slice-start = ((s8[8388608]{0:T(1024)(128)(4,1)}), s8[4194304]{0:T(1024)(128)(4,1)S(1)}, s32[]{:S(2)}) async-start(s8[8388608]{0:T(1024)(128)(4,1)} %bitcast.80), calls=%async_computation.6 | async-start | bytes 8388608
  452.3 3.7 slice-start.1
  468.2 76.7 %copy-start.4 = (f32[64,16,128]{2,1,0:T(8,128)S(1)}, f32[64,16,128]{2,1,0:T(8,128)}, u32[]{:S(2)}) copy-start(f32[64,16,128]{2,1,0:T(8,128)} %param.6) | copy-start | bytes 1572868
Sparse Core Ops, SparseCore 0:
  9.8 57.1 all-gather.2
  104.6 225.2 reduce-scatter.2
  337.2 98.7 all-gather.4
  468.4 74.1 reduce-scatter.4
where the time goes:
time: 554 us; the launch traced here: 553 us
  waiting for transfers between devices  457 us (82%)
  matrix products  44.4 us (8%)
  local copies, waits for them, and re-layouts  31.7 us (6%)
  between operations  14 us (3%)
    reduce_scatter x1, waiting for transfers between devices, per_device(): share = lax.psum_scatter(conv, 'rec', scatter_dimension=3, tiled=True)  224 us
    all_gather x1, waiting for transfers between devices, per_device(): lax.all_gather(spectra(upgoing, cosine, sine), 'rec', axis=3, tiled=True)  98.7 us
    reduce_scatter x1, waiting for transfers between devices, per_device(): lax.psum_scatter(jnp.stack([corr_re, corr_im]), 'src', scatter_dimension=...  74.3 us
    all_gather x1, waiting for transfers between devices, per_device(): traces = lax.all_gather(focusing, 'src', axis=1, tiled=True)  59.1 us
    dot_general x2, matrix products, spectra(): imag_part = -jnp.einsum('pnt,kt->kpn', traces, sine, precision=HIGH)  13.7 us
  transfers between devices with their start and end apart: 4, of which 4 were waited for; matrix products, arithmetic and copies ran while one was open for 0% of the time, Pallas kernels for 0%

commit v1 on v0

--- a/solution.py
+++ b/solution.py
@@ -63,7 +63,12 @@
     start = (src_idx * n_rec + rec_idx) * width
     traces_up = synth(share, cosine, sine, samples)
     upgoing = jnp.where(onset_masked(traces_up, onset, start, width), traces_up, 0.0)
-    upgoing_spectrum = lax.all_gather(spectra(upgoing, cosine, sine), "rec", axis=3, tiled=True)
+    upgoing_spectrum = jnp.concatenate(
+        lax.all_to_all(
+            jnp.stack([spectra(upgoing, cosine, sine)] * lax.axis_size("rec")), "rec", 0, 0
+        ),
+        axis=3,
+    )
     corr_re = jnp.einsum(
         "alt,ath->alh", upgoing_spectrum[0], kernel_real, preferred_element_type=jnp.float32
     ) + jnp.einsum(

time: 554 us -> 512 us (0.924)
  waiting for transfers between devices: 457 us -> 359 us
  blocking collectives: 0 us -> 52.5 us
  local copies, waits for them, and re-layouts: 31.7 us -> 45.1 us
  matrix products: 44.4 us -> 36.3 us
    all_gather x1 -> x0, waiting for transfers between devices: 98.7 us -> none  [per_device(): lax.all_gather(spectra(upgoing, cosine, sine), 'rec', axis=3, tiled=True)]
    all_to_all x0 -> x1, blocking collectives: none -> 52.5 us  [per_device(): lax.all_to_all(jnp.stack([spectra(upgoing, cosine, sine)] * lax.axis_size...]
    unnamed x18 -> x19, local copies, waits for them, and re-layouts: 1.64 us -> 18.3 us
    squeeze x3 -> x0, local copies, waits for them, and re-layouts: 8.76 us -> none  [the longest x2 5.97 us: per_device(): upgoing_spectrum[1]]
  transfers between devices with their start and end apart: 4 -> 3, of which waited for: 4 -> 3; matrix products, arithmetic and copies ran while one was open for 0% -> 0% of each run, Pallas kernels for 0% -> 0%
where the time goes in v1:
time: 512 us
  waiting for transfers between devices  359 us (70%)
  blocking collectives  52.5 us (10%)
  local copies, waits for them, and re-layouts  45.1 us (9%)
  matrix products  36.3 us (7%)
  between operations  14 us (3%)
    reduce_scatter x1, waiting for transfers between devices, per_device(): share = lax.psum_scatter(conv, 'rec', scatter_dimension=3, tiled=True)  224 us
    reduce_scatter x1, waiting for transfers between devices, per_device(): lax.psum_scatter(jnp.stack([corr_re, corr_im]), 'src', scatter_dimension=...  74.8 us
    all_gather x1, waiting for transfers between devices, per_device(): traces = lax.all_gather(focusing, 'src', axis=1, tiled=True)  59.1 us
    all_to_all x1, blocking collectives, per_device(): lax.all_to_all(jnp.stack([spectra(upgoing, cosine, sine)] * lax.axis_size...  52.5 us
    unnamed x19, local copies, waits for them, and re-layouts  18.3 us
    dot_general x2, matrix products, spectra(): imag_part = -jnp.einsum('pnt,kt->kpn', traces, sine, precision=HIGH)  13.7 us
    dot_general x2, matrix products, spectra(): real_part = jnp.einsum('pnt,kt->kpn', traces, cosine, precision=HIGH)  10.4 us
  transfers between devices with their start and end apart: 3, of which 3 were waited for; matrix products, arithmetic and copies ran while one was open for 0% of the time, Pallas kernels for 0%

profile of v1, /device:TPU:32, one launch (start us, length us, event | category | flops | bytes accessed | tf_op | source)
XLA Modules:
  0.0 511.6 jit_solution(7807059555065580149)
XLA Ops:
  7.2 0.0 all-gather.2.cloned.1.call-start
  7.2 0.7 all-gather.2.cloned.1.call-update
  7.9 0.0 reduce-scatter.3.cloned.1.call-start
  8.0 59.1 %all-gather.2.cloned.1.call-done = f32[64,256,128]{2,1,0:T(8,128)} async-done(((f32[64,16,128]{2,1,0:T(8,128)}), f32[64,256,128]{2,1,0:T(8,128)}) %all-gather.2.cloned.1.call-update) | async-done | bytes 8388624 | tf_op jit(solution)/shard_map/all_gather | solution.py:47
  67.0 12.0 %negate_convert_fusion = bf16[32,64,256]{2,0,1:T(8,128)(2,1)S(1)} fusion(f32[64,256,128]{2,1,0:T(8,128)} %all-gather.2.cloned.1.call-done, s32[32]{0:T(128)S(1)} %iota_add_fusion), kind=kOutput, calls=%fused_computation.30 | convolution fusion | flops 806412288 | bytes 9437312 | tf_op jit(solution)/shard_map/pnt,kt->kpn/dot_general | solution.py:21
  79.1 1.3 fusion.6
  80.3 8.8 %convolution_convert_fusion = bf16[32,64,256]{2,0,1:T(8,128)(2,1)S(1)} fusion(f32[64,256,128]{2,1,0:T(8,128)S(1)} %copy-done.1, s32[32]{0:T(128)S(1)} %iota_add_fusion), kind=kOutput, calls=%fused_computation.31 | convolution fusion | flops 805888000 | bytes 9437312 | tf_op jit(solution)/shard_map/pnt,kt->kpn/dot_general | solution.py:20
  89.1 1.3 fusion.4
  90.4 1.3 subtract_bitcast_fusion.1
  91.7 1.3 add_bitcast_fusion.1
  93.0 2.2 pad_maximum_fusion
  95.3 9.2 %copy.36 = f32[2,32,64,256]{2,1,0,3:T(8,128)} copy(f32[2,32,64,256]{3,2,1,0:T(8,128)} %pad_maximum_fusion) | data formatting | bytes 8388608 | tf_op jit(solution)/shard_map/stack | solution.py:61
  104.4 0.0 reduce-scatter.3.cloned.1.call-update
  104.5 0.0 reduce-scatter.5.cloned.1.call-start
  104.5 0.9 constant_dynamic-slice_fusion
  105.4 224.5 %reduce-scatter.3.cloned.1.call-done = f32[2,32,64,16]{2,1,0,3:T(8,128)} async-done(((f32[2,32,64,256]{2,1,0,3:T(8,128)}), f32[2,32,64,16]{2,1,0,3:T(8,128)}) %reduce-scatter.3.cloned.1.call-update) | async-done | bytes 262160 | tf_op jit(solution)/shard_map/reduce_scatter | solution.py:62
  329.8 1.1 fusion.115
  330.9 0.3 copy.55
  331.2 0.7 fusion.48
  331.9 0.3 copy.56
  332.2 0.7 fusion.36
  332.9 1.6 fusion.38
  334.6 1.6 fusion.39
  336.2 0.1 pad_maximum_fusion.2
  336.3 0.1 copy.41
  336.4 2.9 broadcast_bitcast_fusion
  339.3 6.3 %reshape.40 = bf16[16,2,32768]{2,1,0:T(2,128)(2,1)S(1)} reshape(bf16[16,2,32,16,64]{4,3,2,1,0:T(8,128)(2,1)} %broadcast_bitcast_fusion) | data formatting | bytes 4194304
  345.6 52.5 %all_to_all.5 = bf16[16,2,32768]{2,1,0:T(2,128)(2,1)} all-to-all(bf16[16,2,32768]{2,1,0:T(2,128)(2,1)S(1)} %reshape.40), channel_id=1, replica_groups=mesh['src'=16,'rec'=16] {'rec'}, dimensions={0} | all-to-all | bytes 4194304 | tf_op jit(solution)/shard_map/all_to_all | solution.py:67
  398.2 7.4 %reshape.41 = bf16[16,2,32,16,64]{4,3,2,1,0:T(8,128)(2,1)} reshape(bf16[16,2,32768]{2,1,0:T(2,128)(2,1)} %all_to_all.5) | data formatting | bytes 4194304
  405.5 3.1 bitcast_bitcast_fusion
  408.7 0.0 slice-start.1
  408.7 1.1 fusion.113
  409.8 0.6 copy.44
  410.4 0.5 slice-done.1
  410.9 0.8 fusion.2
  411.8 0.6 copy.42
  412.4 0.8 fusion
  413.2 0.9 add_bitcast_fusion
  414.1 0.9 subtract_bitcast_fusion
  415.0 2.2 pad_maximum_fusion.1
  417.2 9.2 %copy.48 = f32[2,32,64,256]{2,1,0,3:T(8,128)} copy(f32[2,32,64,256]{3,2,1,0:T(8,128)} %pad_maximum_fusion.1) | data formatting | bytes 8388608 | tf_op jit(solution)/shard_map/stack | solution.py:82
  426.4 0.0 reduce-scatter.5.cloned.1.call-update
  426.4 74.8 %reduce-scatter.5.cloned.1.call-done = f32[2,32,64,16]{2,1,0,3:T(8,128)} async-done(((f32[2,32,64,256]{2,1,0,3:T(8,128)}), f32[2,32,64,16]{2,1,0,3:T(8,128)}) %reduce-scatter.5.cloned.1.call-update) | async-done | bytes 262160 | tf_op jit(solution)/shard_map/reduce_scatter | solution.py:82
  501.2 1.1 fusion.114
  502.3 0.3 copy.57
  502.6 0.3 copy.58
  502.9 0.7 fusion.45
  503.6 1.5 fusion.34
  (13 shorter events, 0.0 us)
Async XLA Ops:
  7.2 59.8 %all-gather.2.cloned.1.call-start = ((), (), s32[]{:S(2)}) async-start(), calls=%async_computation.3 | async-start | bytes 8912896 | tf_op jit(solution)/shard_map/all_gather | solution.py:47
  7.9 322.0 %reduce-scatter.3.cloned.1.call-start = ((), (), s32[]{:S(2)}) async-start(), calls=%async_computation.4 | async-start | bytes 8912896 | tf_op jit(solution)/shard_map/reduce_scatter | solution.py:62
  67.0 12.0 %copy-start = (bf16[2,32,256,256]{3,2,1,0:T(8,128)(2,1)S(1)}, bf16[2,32,256,256]{3,2,1,0:T(8,128)(2,1)}, u32[]{:S(2)}) copy-start(bf16[2,32,256,256]{3,2,1,0:T(8,128)(2,1)} %param.4) | copy-start | bytes 25165828
  67.0 13.3 %copy-start.1 = (f32[64,256,128]{2,1,0:T(8,128)S(1)}, f32[64,256,128]{2,1,0:T(8,128)}, u32[]{:S(2)}) copy-start(f32[64,256,128]{2,1,0:T(8,128)} %all-gather.2.cloned.1.call-done) | copy-start | bytes 25165828
  104.5 396.8 %reduce-scatter.5.cloned.1.call-start = ((), (), s32[]{:S(2)}) async-start(), calls=%async_computation.5 | async-start | bytes 8912896 | tf_op jit(solution)/shard_map/reduce_scatter | solution.py:82
  332.9 12.7 %copy-start.2 = (f32[64,16,128]{2,1,0:T(8,128)}, f32[64,16,128]{2,1,0:T(8,128)S(1)}, u32[]{:S(2)}) copy-start(f32[64,16,128]{2,1,0:T(8,128)S(1)} %fusion.36) | copy-start | bytes 1572868
  405.5 4.9 slice-start
  408.7 2.3 slice-start.1
  426.3 77.2 %copy-start.3 = (f32[64,16,128]{2,1,0:T(8,128)S(1)}, f32[64,16,128]{2,1,0:T(8,128)}, u32[]{:S(2)}) copy-start(f32[64,16,128]{2,1,0:T(8,128)} %param.6) | copy-start | bytes 1572868
Sparse Core Ops, SparseCore 0:
  9.8 57.1 all-gather.1
  104.6 225.2 reduce-scatter.2
  426.5 74.6 reduce-scatter.4
